TPU v7x, 32 devices: a whole 2x2x4 slice. The times are simulated.
32 devices in a mesh: dp: 16 (over z, x, core), tensor: 2 (over y).
Axes of the slice: x: 2, y: 2, z: 4, core: 2. Of those that a mesh axis runs over, the one named last changes fastest.
Arguments:
- features: bfloat16 [512, 16, 4096], P('tensor', 'dp'), may hold values from -6 to 6
- cotangent: bfloat16 [512, 16, 4096], P('tensor', 'dp'), may hold values from -6 to 6
- embedding: bfloat16 [16, 2048], P('dp'), may hold values from -6 to 6
- context: bfloat16 [16, 260, 2048], P('dp'), may hold values from -6 to 6
- lengths: int32 [16], P('dp'), may hold values from 5 to 256, as said below
- norm1_gain: float32 [512], P('tensor'), may hold values from 0.25 to 1.75
- norm1_bias: float32 [512], P('tensor'), may hold values from -2 to 2
- conv1_weight: bfloat16 [512, 4608], P('tensor'), may hold values from -0.09375 to 0.09375
- conv1_bias: float32 [512], P('tensor'), may hold values from -2 to 2
- emb_weight: bfloat16 [2, 2048, 512], P(None, None, 'tensor'), may hold values from -0.125 to 0.125
- emb_bias: float32 [2, 512], P(None, 'tensor'), may hold values from -2 to 2
- norm2_gain: float32 [512], P('tensor'), may hold values from 0.25 to 1.75
- norm2_bias: float32 [512], P('tensor'), may hold values from -2 to 2
- conv2_weight: bfloat16 [512, 4608], P('tensor'), may hold values from -0.09375 to 0.09375
- conv2_bias: float32 [512], P('tensor'), may hold values from -2 to 2
- norm3_gain: float32 [512], P('tensor'), may hold values from 0.25 to 1.75
- norm3_bias: float32 [512], P('tensor'), may hold values from -2 to 2
- qkv_weight: bfloat16 [3, 512, 512], P(None, 'tensor'), may hold values from -0.25 to 0.25
- qkv_bias: float32 [3, 512], P(None, 'tensor'), may hold values from -2 to 2
- context_weight: bfloat16 [2, 512, 2048], P(None, 'tensor'), may hold values from -0.125 to 0.125
- context_bias: float32 [2, 512], P(None, 'tensor'), may hold values from -2 to 2
- out_weight: bfloat16 [512, 512], P('tensor'), may hold values from -2 to 2
- out_bias: float32 [512], P('tensor'), may hold values from -2 to 2
Outputs:
- output: bfloat16 [512, 16, 4096], P('tensor', 'dp')
- input_grad: float32 [512, 16, 4096], P('tensor', 'dp')
- norm1_gain_grad: float32 [512], P('tensor')
- norm1_bias_grad: float32 [512], P('tensor')
- conv1_weight_grad: float32 [512, 4608], P('tensor')
- conv1_bias_grad: float32 [512], P('tensor')
- emb_weight_grad: float32 [2, 2048, 512], P(None, None, 'tensor')
- emb_bias_grad: float32 [2, 512], P(None, 'tensor')
- norm2_gain_grad: float32 [512], P('tensor')
- norm2_bias_grad: float32 [512], P('tensor')
- conv2_weight_grad: float32 [512, 4608], P('tensor')
- conv2_bias_grad: float32 [512], P('tensor')
- norm3_gain_grad: float32 [512], P('tensor')
- norm3_bias_grad: float32 [512], P('tensor')
- qkv_weight_grad: float32 [3, 512, 512], P(None, 'tensor')
- qkv_bias_grad: float32 [3, 512], P(None, 'tensor')
- context_weight_grad: float32 [2, 512, 2048], P(None, 'tensor')
- context_bias_grad: float32 [2, 512], P(None, 'tensor')
- out_weight_grad: float32 [512, 512], P('tensor')
- out_bias_grad: float32 [512], P('tensor')
Inputs may be any that keep to these rules, and one draw needn't show every extreme that they name: `lengths`: each image's number of real text tokens; some image has 256.
All inputs are finite; a program needn't handle non-finite values.
Results may differ from a plain program's by a relative error of at most 0.025.
Values may be sent and summed in bfloat16 or wider, within the bound.
No kernel may reach another device: no remote copies, remote signals or barrier semaphores. Data moves between devices by JAX's collectives and lax.ppermute only.
A program may use at most 384 MiB of HBM per device.

v0:
```python
import jax
import jax.numpy as jnp
from jax import lax
from jax.sharding import PartitionSpec as P

C = 512
HEAD_DIM = 64
GROUPS = 32
SIDE = 64
HW = 4096
CTX = 260
EPSILON = 1e-05
NEG_FILL = -1e30


def group_norm(values, gain_vec, bias_vec):
    channels, images, pixels = values.shape
    per_group = C // GROUPS
    grouped = values.reshape(channels // per_group, per_group, images, pixels)
    group_mean = jnp.mean(grouped, axis=(1, 3), keepdims=True)
    group_var = jnp.mean(jnp.square(grouped - group_mean), axis=(1, 3), keepdims=True)
    normal_vals = ((grouped - group_mean) * lax.rsqrt(group_var + EPSILON)).reshape(values.shape)
    return normal_vals * gain_vec[:, None, None] + bias_vec[:, None, None]


def shifted(values, kernel_tap):
    row_off, col_off = (kernel_tap // 3, kernel_tap % 3)
    channels, images, pixels = values.shape
    padded = jnp.pad(values.reshape(channels, images, SIDE, SIDE), ((0, 0), (0, 0), (1, 1), (1, 1)))
    return padded[:, :, row_off : row_off + SIDE, col_off : col_off + SIDE].reshape(
        channels, images, pixels
    )


def convolve(full_act, weight, bias_vec):
    kernel = weight.reshape(weight.shape[0], 9, C)
    result = (
        jnp.zeros((weight.shape[0],) + full_act.shape[1:], jnp.float32) + bias_vec[:, None, None]
    )
    for kernel_tap in range(9):
        result = result + jnp.einsum(
            "oc,cip->oip",
            kernel[:, kernel_tap],
            shifted(full_act, kernel_tap),
            preferred_element_type=jnp.float32,
        )
    return result


def kernel_grad(grad_low, full_act):
    pieces = [
        jnp.einsum(
            "oip,cip->oc",
            grad_low,
            shifted(full_act, kernel_tap),
            preferred_element_type=jnp.float32,
        )
        for kernel_tap in range(9)
    ]
    return jnp.stack(pieces, axis=1).reshape(grad_low.shape[0], 9 * C)


def conv_input_grad(grad_low, weight):
    channels = grad_low.shape[0]
    kernel = weight.reshape(channels, 9, C)
    moved_grads = [shifted(grad_low, 8 - kernel_tap) for kernel_tap in range(9)]
    result = jnp.zeros((lax.axis_size("tensor") * channels,) + grad_low.shape[1:], jnp.float32)
    for kernel_tap in range(9):
        cols_part = kernel[:, kernel_tap]
        result = result + jnp.einsum(
            "oc,oip->cip", cols_part, moved_grads[kernel_tap], preferred_element_type=jnp.float32
        )
    return lax.psum_scatter(
        result.astype(jnp.bfloat16), "tensor", scatter_dimension=0, tiled=True
    ).astype(jnp.float32)


def to_heads(values):
    channels, images, length_n = values.shape
    return (
        values.reshape(channels // HEAD_DIM, HEAD_DIM, images, length_n)
        .transpose(2, 0, 1, 3)
        .reshape(-1, HEAD_DIM, length_n)
    )


def from_heads(values, images):
    groups_n, head_dims, length_n = values.shape
    heads_here = groups_n // images
    return (
        values.reshape(images, heads_here, head_dims, length_n)
        .transpose(1, 2, 0, 3)
        .reshape(heads_here * head_dims, images, length_n)
    )


def masked_scores(q_block, key_rows, key_valid):
    scores = jnp.einsum(
        "gdi,gdj->gij", q_block, key_rows, preferred_element_type=jnp.float32
    ) * HEAD_DIM ** (-0.5)
    return jnp.where(key_valid[:, None, :], scores, NEG_FILL)


def attend_forward(queries, key_rows, value_rows, key_valid):
    groups_n = queries.shape[0]
    block_len = min(512, HW)
    blocks_q = queries.reshape(groups_n, HEAD_DIM, HW // block_len, block_len).transpose(2, 0, 1, 3)

    def one_block(q_block):
        scores = masked_scores(q_block, key_rows, key_valid)
        row_top = jnp.max(scores, axis=-1, keepdims=True)
        raised = jnp.exp(scores - row_top)
        row_total = jnp.sum(raised, axis=-1, keepdims=True)
        probs_low = (raised / row_total).astype(jnp.bfloat16)
        mixed_out = jnp.einsum(
            "gdj,gij->gdi", value_rows, probs_low, preferred_element_type=jnp.float32
        )
        return (mixed_out.astype(jnp.bfloat16), row_top, row_total)

    mixed_out, row_top, row_total = lax.map(one_block, blocks_q)
    merged = mixed_out.transpose(1, 2, 0, 3).reshape(groups_n, HEAD_DIM, HW)
    return (merged, row_top, row_total)


def attend_backward(queries, key_rows, value_rows, key_valid, grad_mixed, row_top, row_total):
    groups_n = queries.shape[0]
    block_len = min(512, HW)
    count_b = HW // block_len
    blocks_q = queries.reshape(groups_n, HEAD_DIM, count_b, block_len).transpose(2, 0, 1, 3)
    blocks_g = grad_mixed.reshape(groups_n, HEAD_DIM, count_b, block_len).transpose(2, 0, 1, 3)
    scale_val = HEAD_DIM ** (-0.5)

    def one_block(carried, packed):
        key_acc, value_acc = carried
        q_block, g_block, block_top, block_total = packed
        scores = masked_scores(q_block, key_rows, key_valid)
        prob_f32 = jnp.exp(scores - block_top) / block_total
        probs_low = prob_f32.astype(jnp.bfloat16)
        value_acc = value_acc + jnp.einsum(
            "gdi,gij->gdj", g_block, probs_low, preferred_element_type=jnp.float32
        )
        grad_probs = jnp.einsum(
            "gdi,gdj->gij", g_block, value_rows, preferred_element_type=jnp.float32
        )
        delta_row = jnp.sum(prob_f32 * grad_probs, axis=-1, keepdims=True)
        grad_scores = (prob_f32 * (grad_probs - delta_row)).astype(jnp.bfloat16)
        grad_query = (
            jnp.einsum("gij,gdj->gdi", grad_scores, key_rows, preferred_element_type=jnp.float32)
            * scale_val
        )
        key_acc = (
            key_acc
            + jnp.einsum("gij,gdi->gdj", grad_scores, q_block, preferred_element_type=jnp.float32)
            * scale_val
        )
        return ((key_acc, value_acc), grad_query)

    zero_acc = jnp.zeros(key_rows.shape, jnp.float32)
    (key_grad, value_grad), query_grad = lax.scan(
        one_block, (zero_acc, zero_acc), (blocks_q, blocks_g, row_top, row_total)
    )
    query_grad = query_grad.transpose(1, 2, 0, 3).reshape(groups_n, HEAD_DIM, HW)
    return (query_grad, key_grad, value_grad)


def first_section(values, gain_vec, bias_vec):
    return jax.nn.silu(group_norm(values, gain_vec, bias_vec))


def second_section(values, gain_vec, bias_vec, modulation):
    normal_vals = group_norm(values, gain_vec, bias_vec)
    return jax.nn.silu(normal_vals * (1.0 + modulation[0][:, :, None]) + modulation[1][:, :, None])


def local(
    features,
    cotangent,
    embedding,
    context,
    lengths,
    norm1_gain,
    norm1_bias,
    conv1_weight,
    conv1_bias,
    emb_weight,
    emb_bias,
    norm2_gain,
    norm2_bias,
    conv2_weight,
    conv2_bias,
    norm3_gain,
    norm3_bias,
    qkv_weight,
    qkv_bias,
    context_weight,
    context_bias,
    out_weight,
    out_bias,
):
    channels, images, pixels = features.shape
    feat_f32 = features.astype(jnp.float32)
    act_one = first_section(feat_f32, norm1_gain, norm1_bias).astype(jnp.bfloat16)
    full_one = lax.all_gather(act_one, "tensor", axis=0, tiled=True)
    conv_one = convolve(full_one, conv1_weight, conv1_bias)
    emb_act = jax.nn.silu(embedding.astype(jnp.float32)).astype(jnp.bfloat16)
    scale_shift = (
        jnp.einsum("ie,teo->toi", emb_act, emb_weight, preferred_element_type=jnp.float32)
        + emb_bias[:, :, None]
    )
    act_two = second_section(conv_one, norm2_gain, norm2_bias, scale_shift).astype(jnp.bfloat16)
    full_two = lax.all_gather(act_two, "tensor", axis=0, tiled=True)
    hidden = feat_f32 + convolve(full_two, conv2_weight, conv2_bias)
    normed = group_norm(hidden, norm3_gain, norm3_bias).astype(jnp.bfloat16)
    full_three = lax.all_gather(normed, "tensor", axis=0, tiled=True)
    qkv_low = (
        jnp.einsum("toc,cip->toip", qkv_weight, full_three, preferred_element_type=jnp.float32)
        + qkv_bias[:, :, None, None]
    ).astype(jnp.bfloat16)
    ctx_low = (
        jnp.einsum("toe,ine->toin", context_weight, context, preferred_element_type=jnp.float32)
        + context_bias[:, :, None, None]
    ).astype(jnp.bfloat16)
    queries = to_heads(qkv_low[0])
    key_rows = jnp.concatenate([to_heads(qkv_low[1]), to_heads(ctx_low[0])], axis=2)
    value_rows = jnp.concatenate([to_heads(qkv_low[2]), to_heads(ctx_low[1])], axis=2)
    key_limit = HW + 4 + lengths
    key_valid = jnp.repeat(
        jnp.arange(HW + CTX, dtype=jnp.int32)[None, :] < key_limit[:, None],
        channels // HEAD_DIM,
        axis=0,
    )
    heads_mixed, row_top, row_total = attend_forward(queries, key_rows, value_rows, key_valid)
    heads_out = from_heads(heads_mixed, images)
    full_heads = lax.all_gather(heads_out, "tensor", axis=0, tiled=True)
    output = (
        hidden
        + jnp.einsum("oc,cip->oip", out_weight, full_heads, preferred_element_type=jnp.float32)
        + out_bias[:, None, None]
    ).astype(jnp.bfloat16)
    grad_top = cotangent.astype(jnp.float32)
    out_weight_grad = jnp.einsum(
        "oip,cip->oc", cotangent, full_heads, preferred_element_type=jnp.float32
    )
    out_bias_grad = jnp.sum(grad_top, axis=(1, 2))
    cols_part = out_weight
    grad_heads = lax.psum_scatter(
        jnp.einsum("oc,oip->cip", cols_part, cotangent, preferred_element_type=jnp.float32).astype(
            jnp.bfloat16
        ),
        "tensor",
        scatter_dimension=0,
        tiled=True,
    )
    query_grad, key_grad, value_grad = attend_backward(
        queries, key_rows, value_rows, key_valid, to_heads(grad_heads), row_top, row_total
    )
    grad_qkv = jnp.stack(
        [
            from_heads(query_grad, images),
            from_heads(key_grad[:, :, :HW], images),
            from_heads(value_grad[:, :, :HW], images),
        ]
    ).astype(jnp.bfloat16)
    grad_ctx = jnp.stack(
        [from_heads(key_grad[:, :, HW:], images), from_heads(value_grad[:, :, HW:], images)]
    ).astype(jnp.bfloat16)
    qkv_weight_grad = jnp.einsum(
        "toip,cip->toc", grad_qkv, full_three, preferred_element_type=jnp.float32
    )
    qkv_bias_grad = jnp.sum(grad_qkv.astype(jnp.float32), axis=(2, 3))
    context_weight_grad = jnp.einsum(
        "toin,ine->toe", grad_ctx, context, preferred_element_type=jnp.float32
    )
    context_bias_grad = jnp.sum(grad_ctx.astype(jnp.float32), axis=(2, 3))
    cols_part = qkv_weight
    grad_normed = lax.psum_scatter(
        jnp.einsum("toc,toip->cip", cols_part, grad_qkv, preferred_element_type=jnp.float32).astype(
            jnp.bfloat16
        ),
        "tensor",
        scatter_dimension=0,
        tiled=True,
    ).astype(jnp.float32)
    unused_three, pull_three = jax.vjp(group_norm, hidden, norm3_gain, norm3_bias)
    grad_branch, norm3_gain_grad, norm3_bias_grad = pull_three(grad_normed)
    grad_hidden = grad_top + grad_branch
    attention_grads = (
        lax.psum(out_weight_grad.astype(jnp.bfloat16), "dp").astype(jnp.float32),
        lax.psum(out_bias_grad.astype(jnp.bfloat16), "dp").astype(jnp.float32),
        lax.psum(qkv_weight_grad.astype(jnp.bfloat16), "dp").astype(jnp.float32),
        lax.psum(qkv_bias_grad.astype(jnp.bfloat16), "dp").astype(jnp.float32),
        lax.psum(context_weight_grad.astype(jnp.bfloat16), "dp").astype(jnp.float32),
        lax.psum(context_bias_grad.astype(jnp.bfloat16), "dp").astype(jnp.float32),
        lax.psum(norm3_gain_grad.astype(jnp.bfloat16), "dp").astype(jnp.float32),
        lax.psum(norm3_bias_grad.astype(jnp.bfloat16), "dp").astype(jnp.float32),
    )
    grad_conv_two = grad_hidden.astype(jnp.bfloat16)
    conv2_bias_grad = jnp.sum(grad_conv_two.astype(jnp.float32), axis=(1, 2))
    conv2_weight_grad = kernel_grad(grad_conv_two, full_two)
    grad_act_two = conv_input_grad(grad_conv_two, conv2_weight)
    unused_two, pull_two = jax.vjp(second_section, conv_one, norm2_gain, norm2_bias, scale_shift)
    grad_conv_one, norm2_gain_grad, norm2_bias_grad, grad_modulation = pull_two(grad_act_two)
    grad_mod_low = grad_modulation.astype(jnp.bfloat16)
    emb_weight_grad = jnp.einsum(
        "ie,toi->teo", emb_act, grad_mod_low, preferred_element_type=jnp.float32
    )
    emb_bias_grad = jnp.sum(grad_mod_low.astype(jnp.float32), axis=2)
    grad_conv_low = grad_conv_one.astype(jnp.bfloat16)
    conv1_bias_grad = jnp.sum(grad_conv_low.astype(jnp.float32), axis=(1, 2))
    conv1_weight_grad = kernel_grad(grad_conv_low, full_one)
    grad_act_one = conv_input_grad(grad_conv_low, conv1_weight)
    unused_one, pull_one = jax.vjp(first_section, feat_f32, norm1_gain, norm1_bias)
    grad_feat, norm1_gain_grad, norm1_bias_grad = pull_one(grad_act_one)
    input_grad = grad_hidden + grad_feat
    residual_grads = (
        lax.psum(norm1_gain_grad.astype(jnp.bfloat16), "dp").astype(jnp.float32),
        lax.psum(norm1_bias_grad.astype(jnp.bfloat16), "dp").astype(jnp.float32),
        lax.psum(conv1_weight_grad.astype(jnp.bfloat16), "dp").astype(jnp.float32),
        lax.psum(conv1_bias_grad.astype(jnp.bfloat16), "dp").astype(jnp.float32),
        lax.psum(emb_weight_grad.astype(jnp.bfloat16), "dp").astype(jnp.float32),
        lax.psum(emb_bias_grad.astype(jnp.bfloat16), "dp").astype(jnp.float32),
        lax.psum(norm2_gain_grad.astype(jnp.bfloat16), "dp").astype(jnp.float32),
        lax.psum(norm2_bias_grad.astype(jnp.bfloat16), "dp").astype(jnp.float32),
        lax.psum(conv2_weight_grad.astype(jnp.bfloat16), "dp").astype(jnp.float32),
        lax.psum(conv2_bias_grad.astype(jnp.bfloat16), "dp").astype(jnp.float32),
    )
    return (
        output,
        input_grad,
        residual_grads[0],
        residual_grads[1],
        residual_grads[2],
        residual_grads[3],
        residual_grads[4],
        residual_grads[5],
        residual_grads[6],
        residual_grads[7],
        residual_grads[8],
        residual_grads[9],
        attention_grads[6],
        attention_grads[7],
        attention_grads[2],
        attention_grads[3],
        attention_grads[4],
        attention_grads[5],
        attention_grads[0],
        attention_grads[1],
    )


def solution(mesh):
    placed = (
        P("tensor", "dp", None),
        P("tensor", "dp", None),
        P("dp", None),
        P("dp", None, None),
        P("dp"),
        P("tensor"),
        P("tensor"),
        P("tensor", None),
        P("tensor"),
        P(None, None, "tensor"),
        P(None, "tensor"),
        P("tensor"),
        P("tensor"),
        P("tensor", None),
        P("tensor"),
        P("tensor"),
        P("tensor"),
        P(None, "tensor", None),
        P(None, "tensor"),
        P(None, "tensor", None),
        P(None, "tensor"),
        P("tensor", None),
        P("tensor"),
    )
    return jax.shard_map(
        local,
        mesh=mesh,
        in_specs=placed,
        out_specs=(
            P("tensor", "dp", None),
            P("tensor", "dp", None),
            P("tensor"),
            P("tensor"),
            P("tensor", None),
            P("tensor"),
            P(None, None, "tensor"),
            P(None, "tensor"),
            P("tensor"),
            P("tensor"),
            P("tensor", None),
            P("tensor"),
            P("tensor"),
            P("tensor"),
            P(None, "tensor", None),
            P(None, "tensor"),
            P(None, "tensor", None),
            P(None, "tensor"),
            P("tensor", None),
            P("tensor"),
        ),
        check_vma=False,
    )
```

profile of v0, /device:TPU:0, one launch (start us, length us, event | category | flops | bytes accessed | tf_op | source)
XLA Modules:
  0.0 2261.5 jit_solution(17377600485982242379)
XLA Ops:
  27.8 53.2 %all-gather.6.cloned.1.call-done = bf16[512,1,4096]{0,2,1:T(8,128)(2,1)} async-done(((bf16[256,1,4096]{0,2,1:T(8,128)(2,1)}), bf16[512,1,4096]{0,2,1:T(8,128)(2,1)}) %all-gather.6.cloned.1.call-update) | async-done | bytes 4194320 | tf_op jit(solution)/shard_map/all_gather | solution.py:203
  81.0 22.1 pad_slice_fusion.8
  147.0 47.4 %all-gather.12.cloned.1.call-done = bf16[512,4096]{0,1:T(8,128)(2,1)} async-done(((bf16[256,4096]{0,1:T(8,128)(2,1)}), bf16[512,4096]{0,1:T(8,128)(2,1)}) %all-gather.12.cloned.1.call-update) | async-done | bytes 4194320 | tf_op jit(solution)/shard_map/all_gather | solution.py:211
  194.5 21.5 pad_slice_fusion
  257.5 51.8 %all-gather.8.cloned.1.call-done = bf16[512,1,4096]{0,2,1:T(8,128)(2,1)} async-done(((bf16[256,1,4096]{0,2,1:T(8,128)(2,1)}), bf16[512,1,4096]{0,2,1:T(8,128)(2,1)}) %all-gather.8.cloned.1.call-update) | async-done | bytes 4194320 | tf_op jit(solution)/shard_map/all_gather | solution.py:214
  322.8 393.9 %while.30 = (s32[]{:T(128)}, bf16[8,4,64,512]{3,2,1,0:T(8,128)(2,1)}, f32[8,4,512,1]{2,1,3,0:T(4,128)S(1)}, f32[8,4,512,1]{2,1,3,0:T(4,128)S(1)}, bf16[8,4,64,51...) while((s32[]{:T(128)}, ...), condition=%wide.region_15.16_spmd.clone, body=%wide.region_12.15_spmd.clone.sunk | while | flops 2390978560 | bytes 121079936 | solution.py:120
  322.8 16.9 fusion.444
  372.0 16.9 fusion.444
  421.3 16.9 fusion.444
  519.7 16.9 fusion.444
  716.7 922.0 %while.31 = (s32[]{:T(128)}, f32[4,64,4356]{2,1,0:T(8,128)}, f32[4,64,4356]{2,1,0:T(8,128)}, bf16[8,4,64,512]{3,2,1,0:T(8,128)(2,1)}, bf16[8,4,64,512]{3,2,1,0:T...) while((s32[]{:T(128)}, f32[4,64,4356]{2,1,0:T(8,128)}, ...), condition=%wide.region_19.20_spmd.clone, body=%wide.region_17.19_spmd.clone.sunk | while | flops 5804411904 | bytes 302971552 | solution.py:159
  716.8 18.3 fusion.456
  735.2 30.3 %multiply_reduce_fusion.7 = (f32[4,512]{1,0:T(4,128)S(1)}, f32[4,512,4356]{1,2,0:T(8,128)}) fusion(f32[4,512,4356]{1,2,0:T(8,128)} %fusion.456, f32[4,512]{1,0:T(4,128)S(1)} %get-tuple-element.508, f32[4,512]{1,0:T(4,128)S(1)} %get-tuple-element.509, bf16[4,64,4356]{2,1,0:T(8,128)(2,1)} %get-tuple-element.570, ...), kind=kOutput, calls=%fused_computation.20.clone.1 | convolution fusion | flops 1195423744 | bytes 73890816 | tf_op jit(solution)/shard_map/while/body/eval_jaxpr/gdi,gdj->gij/dot_general | solution.py:98
  765.5 29.7 %multiply_convert_fusion.4 = bf16[4,512,4356]{1,2,0:T(8,128)(2,1)} fusion(f32[4,512,4356]{1,2,0:T(8,128)} %get-tuple-element.510, f32[4,512,4356]{1,2,0:T(8,128)} %fusion.456, f32[4,512]{1,0:T(4,128)S(1)} %get-tuple-element.511), kind=kLoop, calls=%fused_computation.19.clone.1 | loop fusion | flops 26763264 | bytes 89219072 | tf_op jit(solution)/shard_map/while/body/eval_jaxpr/convert_element_type | solution.py:146
  829.5 18.3 fusion.456
  847.9 30.3 %multiply_reduce_fusion.7 = (f32[4,512]{1,0:T(4,128)S(1)}, f32[4,512,4356]{1,2,0:T(8,128)}) fusion(f32[4,512,4356]{1,2,0:T(8,128)} %fusion.456, f32[4,512]{1,0:T(4,128)S(1)} %get-tuple-element.508, f32[4,512]{1,0:T(4,128)S(1)} %get-tuple-element.509, bf16[4,64,4356]{2,1,0:T(8,128)(2,1)} %get-tuple-element.570, ...), kind=kOutput, calls=%fused_computation.20.clone.1 | convolution fusion | flops 1195423744 | bytes 73890816 | tf_op jit(solution)/shard_map/while/body/eval_jaxpr/gdi,gdj->gij/dot_general | solution.py:98
  878.1 29.7 %multiply_convert_fusion.4 = bf16[4,512,4356]{1,2,0:T(8,128)(2,1)} fusion(f32[4,512,4356]{1,2,0:T(8,128)} %get-tuple-element.510, f32[4,512,4356]{1,2,0:T(8,128)} %fusion.456, f32[4,512]{1,0:T(4,128)S(1)} %get-tuple-element.511), kind=kLoop, calls=%fused_computation.19.clone.1 | loop fusion | flops 26763264 | bytes 89219072 | tf_op jit(solution)/shard_map/while/body/eval_jaxpr/convert_element_type | solution.py:146
  928.1 17.0 fusion.458
  945.1 18.3 fusion.456
  963.4 30.3 %multiply_reduce_fusion.7 = (f32[4,512]{1,0:T(4,128)S(1)}, f32[4,512,4356]{1,2,0:T(8,128)}) fusion(f32[4,512,4356]{1,2,0:T(8,128)} %fusion.456, f32[4,512]{1,0:T(4,128)S(1)} %get-tuple-element.508, f32[4,512]{1,0:T(4,128)S(1)} %get-tuple-element.509, bf16[4,64,4356]{2,1,0:T(8,128)(2,1)} %get-tuple-element.570, ...), kind=kOutput, calls=%fused_computation.20.clone.1 | convolution fusion | flops 1195423744 | bytes 73890816 | tf_op jit(solution)/shard_map/while/body/eval_jaxpr/gdi,gdj->gij/dot_general | solution.py:98
  993.7 29.7 %multiply_convert_fusion.4 = bf16[4,512,4356]{1,2,0:T(8,128)(2,1)} fusion(f32[4,512,4356]{1,2,0:T(8,128)} %get-tuple-element.510, f32[4,512,4356]{1,2,0:T(8,128)} %fusion.456, f32[4,512]{1,0:T(4,128)S(1)} %get-tuple-element.511), kind=kLoop, calls=%fused_computation.19.clone.1 | loop fusion | flops 26763264 | bytes 89219072 | tf_op jit(solution)/shard_map/while/body/eval_jaxpr/convert_element_type | solution.py:146
  1043.6 17.0 fusion.458
  1060.6 18.3 fusion.456
  1079.0 30.3 %multiply_reduce_fusion.7 = (f32[4,512]{1,0:T(4,128)S(1)}, f32[4,512,4356]{1,2,0:T(8,128)}) fusion(f32[4,512,4356]{1,2,0:T(8,128)} %fusion.456, f32[4,512]{1,0:T(4,128)S(1)} %get-tuple-element.508, f32[4,512]{1,0:T(4,128)S(1)} %get-tuple-element.509, bf16[4,64,4356]{2,1,0:T(8,128)(2,1)} %get-tuple-element.570, ...), kind=kOutput, calls=%fused_computation.20.clone.1 | convolution fusion | flops 1195423744 | bytes 73890816 | tf_op jit(solution)/shard_map/while/body/eval_jaxpr/gdi,gdj->gij/dot_general | solution.py:98
  1109.2 29.7 %multiply_convert_fusion.4 = bf16[4,512,4356]{1,2,0:T(8,128)(2,1)} fusion(f32[4,512,4356]{1,2,0:T(8,128)} %get-tuple-element.510, f32[4,512,4356]{1,2,0:T(8,128)} %fusion.456, f32[4,512]{1,0:T(4,128)S(1)} %get-tuple-element.511), kind=kLoop, calls=%fused_computation.19.clone.1 | loop fusion | flops 26763264 | bytes 89219072 | tf_op jit(solution)/shard_map/while/body/eval_jaxpr/convert_element_type | solution.py:146
  1159.2 17.0 fusion.458
  1176.2 18.3 fusion.456
  1194.5 30.3 %multiply_reduce_fusion.7 = (f32[4,512]{1,0:T(4,128)S(1)}, f32[4,512,4356]{1,2,0:T(8,128)}) fusion(f32[4,512,4356]{1,2,0:T(8,128)} %fusion.456, f32[4,512]{1,0:T(4,128)S(1)} %get-tuple-element.508, f32[4,512]{1,0:T(4,128)S(1)} %get-tuple-element.509, bf16[4,64,4356]{2,1,0:T(8,128)(2,1)} %get-tuple-element.570, ...), kind=kOutput, calls=%fused_computation.20.clone.1 | convolution fusion | flops 1195423744 | bytes 73890816 | tf_op jit(solution)/shard_map/while/body/eval_jaxpr/gdi,gdj->gij/dot_general | solution.py:98
  1224.8 29.7 %multiply_convert_fusion.4 = bf16[4,512,4356]{1,2,0:T(8,128)(2,1)} fusion(f32[4,512,4356]{1,2,0:T(8,128)} %get-tuple-element.510, f32[4,512,4356]{1,2,0:T(8,128)} %fusion.456, f32[4,512]{1,0:T(4,128)S(1)} %get-tuple-element.511), kind=kLoop, calls=%fused_computation.19.clone.1 | loop fusion | flops 26763264 | bytes 89219072 | tf_op jit(solution)/shard_map/while/body/eval_jaxpr/convert_element_type | solution.py:146
  1274.7 17.0 fusion.458
  1291.7 18.3 fusion.456
  1310.1 30.3 %multiply_reduce_fusion.7 = (f32[4,512]{1,0:T(4,128)S(1)}, f32[4,512,4356]{1,2,0:T(8,128)}) fusion(f32[4,512,4356]{1,2,0:T(8,128)} %fusion.456, f32[4,512]{1,0:T(4,128)S(1)} %get-tuple-element.508, f32[4,512]{1,0:T(4,128)S(1)} %get-tuple-element.509, bf16[4,64,4356]{2,1,0:T(8,128)(2,1)} %get-tuple-element.570, ...), kind=kOutput, calls=%fused_computation.20.clone.1 | convolution fusion | flops 1195423744 | bytes 73890816 | tf_op jit(solution)/shard_map/while/body/eval_jaxpr/gdi,gdj->gij/dot_general | solution.py:98
  1340.3 29.7 %multiply_convert_fusion.4 = bf16[4,512,4356]{1,2,0:T(8,128)(2,1)} fusion(f32[4,512,4356]{1,2,0:T(8,128)} %get-tuple-element.510, f32[4,512,4356]{1,2,0:T(8,128)} %fusion.456, f32[4,512]{1,0:T(4,128)S(1)} %get-tuple-element.511), kind=kLoop, calls=%fused_computation.19.clone.1 | loop fusion | flops 26763264 | bytes 89219072 | tf_op jit(solution)/shard_map/while/body/eval_jaxpr/convert_element_type | solution.py:146
  1390.2 17.0 fusion.458
  1407.2 18.3 fusion.456
  1425.6 30.3 %multiply_reduce_fusion.7 = (f32[4,512]{1,0:T(4,128)S(1)}, f32[4,512,4356]{1,2,0:T(8,128)}) fusion(f32[4,512,4356]{1,2,0:T(8,128)} %fusion.456, f32[4,512]{1,0:T(4,128)S(1)} %get-tuple-element.508, f32[4,512]{1,0:T(4,128)S(1)} %get-tuple-element.509, bf16[4,64,4356]{2,1,0:T(8,128)(2,1)} %get-tuple-element.570, ...), kind=kOutput, calls=%fused_computation.20.clone.1 | convolution fusion | flops 1195423744 | bytes 73890816 | tf_op jit(solution)/shard_map/while/body/eval_jaxpr/gdi,gdj->gij/dot_general | solution.py:98
  1455.9 29.7 %multiply_convert_fusion.4 = bf16[4,512,4356]{1,2,0:T(8,128)(2,1)} fusion(f32[4,512,4356]{1,2,0:T(8,128)} %get-tuple-element.510, f32[4,512,4356]{1,2,0:T(8,128)} %fusion.456, f32[4,512]{1,0:T(4,128)S(1)} %get-tuple-element.511), kind=kLoop, calls=%fused_computation.19.clone.1 | loop fusion | flops 26763264 | bytes 89219072 | tf_op jit(solution)/shard_map/while/body/eval_jaxpr/convert_element_type | solution.py:146
  1505.8 17.0 fusion.458
  1522.8 18.3 fusion.456
  1541.1 30.3 %multiply_reduce_fusion.7 = (f32[4,512]{1,0:T(4,128)S(1)}, f32[4,512,4356]{1,2,0:T(8,128)}) fusion(f32[4,512,4356]{1,2,0:T(8,128)} %fusion.456, f32[4,512]{1,0:T(4,128)S(1)} %get-tuple-element.508, f32[4,512]{1,0:T(4,128)S(1)} %get-tuple-element.509, bf16[4,64,4356]{2,1,0:T(8,128)(2,1)} %get-tuple-element.570, ...), kind=kOutput, calls=%fused_computation.20.clone.1 | convolution fusion | flops 1195423744 | bytes 73890816 | tf_op jit(solution)/shard_map/while/body/eval_jaxpr/gdi,gdj->gij/dot_general | solution.py:98
  1571.4 29.7 %multiply_convert_fusion.4 = bf16[4,512,4356]{1,2,0:T(8,128)(2,1)} fusion(f32[4,512,4356]{1,2,0:T(8,128)} %get-tuple-element.510, f32[4,512,4356]{1,2,0:T(8,128)} %fusion.456, f32[4,512]{1,0:T(4,128)S(1)} %get-tuple-element.511), kind=kLoop, calls=%fused_computation.19.clone.1 | loop fusion | flops 26763264 | bytes 89219072 | tf_op jit(solution)/shard_map/while/body/eval_jaxpr/convert_element_type | solution.py:146
  1621.3 17.0 fusion.458
  1683.3 45.2 %reduce-scatter.7.cloned.1.call-done = bf16[256,1,4096]{0,2,1:T(8,128)(2,1)} async-done(((bf16[512,1,4096]{0,2,1:T(8,128)(2,1)}), bf16[256,1,4096]{0,2,1:T(8,128)(2,1)}) %reduce-scatter.7.cloned.1.call-update) | async-done | bytes 2097168 | tf_op jit(solution)/shard_map/reduce_scatter | solution.py:276
  1789.2 24.4 %fusion.43 = bf16[512,1,4096]{0,2,1:T(8,128)(2,1)} fusion(bf16[256,4096]{0,1:T(8,128)(2,1)} %bitcast.785, f32[4096,512]{1,0:T(8,128)} %fusion.338, f32[4096,512]{1,0:T(8,128)} %fusion.337, f32[4096,512]{1,0:T(8,128)} %fusion.336, f32[4096,512]{1,0:T(8,128)} %fusion.133, f32[4096,512]{1,0:T(8,128)} %fusion.335, f32[4096,512]{1,0:T(8,128)} %fusion.334, ...), kind=kOutput, calls=%fused_computation.63 | convolution fusion | flops 1092616192 | bytes 73662464 | tf_op jit(solution)/shard_map/oc,oip->cip/dot_general | solution.py:70
  1965.8 25.2 %fusion.44 = bf16[512,1,4096]{0,2,1:T(8,128)(2,1)} fusion(bf16[256,4096]{0,1:T(8,128)(2,1)} %bitcast.784, f32[4096,512]{1,0:T(8,128)} %fusion.331, f32[4096,512]{1,0:T(8,128)} %fusion.330, f32[4096,512]{1,0:T(8,128)} %fusion.329, f32[4096,512]{1,0:T(8,128)} %fusion.113, f32[4096,512]{1,0:T(8,128)} %fusion.328, f32[4096,512]{1,0:T(8,128)} %fusion.327, ...), kind=kOutput, calls=%fused_computation.64 | convolution fusion | flops 1092616192 | bytes 73662464 | tf_op jit(solution)/shard_map/oc,oip->cip/dot_general | solution.py:70
  2012.0 119.1 %all-reduce.10.cloned.1.call-done = (bf16[256,4608]{0,1:T(8,128)(2,1)}, bf16[256,4608]{0,1:T(8,128)(2,1)}, bf16[256,512]{0,1:T(8,128)(2,1)}, bf16[2,2048,256]{2,...) async-done(((bf16[256,4608]{0,1:T(8,128)(2,1)}, bf16[256,4608]{0,1:T(8,128)(2,1)}, bf16[256,512]{0,1:T(8,128)(2,1)}, ...) | async-done | bytes 9961488 | tf_op jit(solution)/shard_map/psum | solution.py:318
  2147.7 40.5 %reduce-scatter.11.cloned.1.call-done = bf16[256,1,4096]{0,2,1:T(8,128)(2,1)} async-done(((bf16[512,1,4096]{0,2,1:T(8,128)(2,1)}), bf16[256,1,4096]{0,2,1:T(8,128)(2,1)}) %reduce-scatter.11.cloned.1.call-update) | async-done | bytes 2097168 | tf_op jit(solution)/shard_map/reduce_scatter | solution.py:73
  2194.1 34.2 %all-reduce.6 = (bf16[256]{0:T(256)(128)(2,1)S(1)}, bf16[256]{0:T(256)(128)(2,1)S(1)}, bf16[256]{0:T(256)(128)(2,1)S(1)}, bf16[2,256]{1,0:T(2,128)(2,1)S(1)}, bf...) all-reduce(bf16[256]{0:T(256)(128)(2,1)S(1)} %get-tuple-element.252, ...), channel_id=1, replica_groups=mesh['dp'=16,'tensor'=2] {'dp'}, use_global_device_ids=true, to_apply=%region_42.43 | all-reduce | flops 4096 | bytes 16384 | tf_op jit(solution)/shard_map/psum | solution.py:316
  (539 shorter events, 946.4 us)
Async XLA Ops:
  7.2 243.3 %copy-start = (bf16[2,256,2048]{2,1,0:T(8,128)(2,1)S(1)}, bf16[2,256,2048]{2,1,0:T(8,128)(2,1)}, u32[]{:S(2)}) copy-start(bf16[2,256,2048]{2,1,0:T(8,128)(2,1)} %param.46) | copy-start | bytes 6291460
  7.2 73.8 %all-gather.6.cloned.1.call-start = ((), (), s32[]{:S(2)}) async-start(), calls=%async_computation.4 | async-start | bytes 6291456 | tf_op jit(solution)/shard_map/all_gather | solution.py:203
  21.5 173.0 %all-gather.12.cloned.1.call-start = ((), (), s32[]{:S(2)}) async-start(), calls=%async_computation.11 | async-start | bytes 6291456 | tf_op jit(solution)/shard_map/all_gather | solution.py:211
  27.8 104.4 %copy-start.72 = (f32[1,256]{1,0:T(1,128)}, f32[1,256]{1,0:T(1,128)S(1)}, u32[]{:S(2)}) copy-start(f32[1,256]{1,0:T(1,128)S(1)} %get-tuple-element.370) | copy-start | bytes 3076
  27.8 104.4 %copy-start.88 = (f32[1,256]{1,0:T(1,128)}, f32[1,256]{1,0:T(1,128)S(1)}, u32[]{:S(2)}) copy-start(f32[1,256]{1,0:T(1,128)S(1)} %get-tuple-element.371) | copy-start | bytes 3076
  81.0 22.1 copy-start.97
  103.1 17.8 copy-start.17
  103.1 19.1 copy-start.15
  103.1 20.5 copy-start.13
  103.1 21.8 copy-start.11
  137.6 116.1 %reduce-scatter.5.cloned.1.call-start = ((), (), s32[]{:S(2)}) async-start(), calls=%async_computation.7 | async-start | bytes 6291456 | tf_op jit(solution)/shard_map/reduce_scatter | solution.py:246
  142.5 166.8 %all-gather.8.cloned.1.call-start = ((), (), s32[]{:S(2)}) async-start(), calls=%async_computation.5 | async-start | bytes 6291456 | tf_op jit(solution)/shard_map/all_gather | solution.py:214
  194.5 21.6 copy-start.98
  216.0 18.1 copy-start.31
  216.0 19.5 copy-start.29
  216.0 20.8 copy-start.27
  216.0 22.1 copy-start.7
  250.3 1478.1 %reduce-scatter.7.cloned.1.call-start = ((), (), s32[]{:S(2)}) async-start(), calls=%async_computation.8 | async-start | bytes 6291456 | tf_op jit(solution)/shard_map/reduce_scatter | solution.py:276
  250.5 58.8 %copy-start.110 = (bf16[3,256,512]{2,1,0:T(8,128)(2,1)S(1)}, bf16[3,256,512]{2,1,0:T(8,128)(2,1)}, u32[]{:S(2)}) copy-start(bf16[3,256,512]{2,1,0:T(8,128)(2,1)} %param.44) | copy-start | bytes 2359300
  250.5 58.8 %copy-start.112 = (f32[3,256]{1,0:T(4,128)S(1)}, f32[3,256]{1,0:T(4,128)}, u32[]{:S(2)}) copy-start(f32[3,256]{1,0:T(4,128)} %param.45) | copy-start | bytes 9220
  339.7 16.3 copy-start.6
  438.2 16.3 copy-start.6
  487.4 16.3 copy-start.6
  536.7 16.3 copy-start.6
  1674.0 154.9 %all-gather.10.cloned.1.call-start = ((), (), s32[]{:S(2)}) async-start(), calls=%async_computation.6 | async-start | bytes 6291456 | tf_op jit(solution)/shard_map/all_gather | solution.py:234
  1680.8 47.7 %copy-start.62 = (f32[256]{0:T(256)S(1)}, f32[256]{0:T(256)}, u32[]{:S(2)}) copy-start(f32[256]{0:T(256)} %copy-done.61) | copy-start | bytes 3076
  1680.8 47.7 %copy-start.75 = (f32[256]{0:T(256)S(1)}, f32[256]{0:T(256)}, u32[]{:S(2)}) copy-start(f32[256]{0:T(256)} %copy-done.74) | copy-start | bytes 3076
  1680.8 47.7 %copy-start.84 = (f32[256]{0:T(256)S(1)}, f32[256]{0:T(256)}, u32[]{:S(2)}) copy-start(f32[256]{0:T(256)} %param.42) | copy-start | bytes 3076
  1683.2 50.2 %copy-start.109 = (f32[16]{0:T(128)S(1)}, f32[16]{0:T(128)}, u32[]{:S(2)}) copy-start(f32[16]{0:T(128)} %copy-done.108) | copy-start | bytes 196
  1683.2 185.0 %reduce-scatter.9.cloned.1.call-start = ((), (), s32[]{:S(2)}) async-start(), calls=%async_computation.9 | async-start | bytes 6291456 | tf_op jit(solution)/shard_map/reduce_scatter | solution.py:73
  1813.6 317.5 %all-reduce.10.cloned.1.call-start = ((), (), s32[]{:S(2)}) async-start(), calls=%async_computation.12 | async-start | bytes 19922944 | tf_op jit(solution)/shard_map/psum | solution.py:318
  1859.0 16.7 copy-start.107
  1935.5 252.7 %reduce-scatter.11.cloned.1.call-start = ((), (), s32[]{:S(2)}) async-start(), calls=%async_computation.10 | async-start | bytes 6291456 | tf_op jit(solution)/shard_map/reduce_scatter | solution.py:73
  2142.7 45.5 %copy-start.5 = (bf16[256,1,4096]{0,2,1:T(8,128)(2,1)S(1)}, bf16[256,1,4096]{0,2,1:T(8,128)(2,1)}, u32[]{:S(2)}) copy-start(bf16[256,1,4096]{0,2,1:T(8,128)(2,1)} %copy.104) | copy-start | bytes 6291460
  2142.8 45.5 %copy-start.65 = (f32[256]{0:T(256)S(1)}, f32[256]{0:T(256)}, u32[]{:S(2)}) copy-start(f32[256]{0:T(256)} %copy-done.64) | copy-start | bytes 3076
  2142.8 45.5 %copy-start.78 = (f32[256]{0:T(256)S(1)}, f32[256]{0:T(256)}, u32[]{:S(2)}) copy-start(f32[256]{0:T(256)} %copy-done.77) | copy-start | bytes 3076
  2142.8 45.5 %copy-start.87 = (f32[256]{0:T(256)S(1)}, f32[256]{0:T(256)}, u32[]{:S(2)}) copy-start(f32[256]{0:T(256)} %param.32) | copy-start | bytes 3076
  2142.8 45.5 %copy-start.96 = (f32[256]{0:T(256)S(1)}, f32[256]{0:T(256)}, u32[]{:S(2)}) copy-start(f32[256]{0:T(256)} %param.33) | copy-start | bytes 3076
  2147.6 46.5 %copy-start.99 = (bf16[256]{0:T(256)(128)(2,1)S(1)}, bf16[256]{0:T(256)(128)(2,1)}, u32[]{:S(2)}) copy-start(bf16[256]{0:T(256)(128)(2,1)} %get-tuple-element.250) | copy-start | bytes 1540
  2147.6 46.5 %copy-start.101 = (bf16[256]{0:T(256)(128)(2,1)S(1)}, bf16[256]{0:T(256)(128)(2,1)}, u32[]{:S(2)}) copy-start(bf16[256]{0:T(256)(128)(2,1)} %get-tuple-element.318) | copy-start | bytes 1540
  2147.6 46.5 %copy-start.102 = (bf16[256]{0:T(256)(128)(2,1)S(1)}, bf16[256]{0:T(256)(128)(2,1)}, u32[]{:S(2)}) copy-start(bf16[256]{0:T(256)(128)(2,1)} %get-tuple-element.351) | copy-start | bytes 1540
  2147.6 87.7 %copy-start.105 = (f32[16]{0:T(128)S(1)}, f32[16]{0:T(128)}, u32[]{:S(2)}) copy-start(f32[16]{0:T(128)} %copy-done.104) | copy-start | bytes 196
  2147.6 89.0 %copy-start.63 = (f32[256]{0:T(256)S(1)}, f32[256]{0:T(256)}, u32[]{:S(2)}) copy-start(f32[256]{0:T(256)} %copy-done.61) | copy-start | bytes 3076
  2147.6 89.0 %copy-start.76 = (f32[256]{0:T(256)S(1)}, f32[256]{0:T(256)}, u32[]{:S(2)}) copy-start(f32[256]{0:T(256)} %copy-done.74) | copy-start | bytes 3076
  2147.7 89.0 %copy-start.82 = (f32[256]{0:T(256)S(1)}, f32[256]{0:T(256)}, u32[]{:S(2)}) copy-start(f32[256]{0:T(256)} %copy-done.81) | copy-start | bytes 3076
  2147.7 89.0 %copy-start.85 = (f32[256]{0:T(256)S(1)}, f32[256]{0:T(256)}, u32[]{:S(2)}) copy-start(f32[256]{0:T(256)} %param.42) | copy-start | bytes 3076
  2147.7 89.0 %copy-start.91 = (f32[256]{0:T(256)S(1)}, f32[256]{0:T(256)}, u32[]{:S(2)}) copy-start(f32[256]{0:T(256)} %copy-done.90) | copy-start | bytes 3076
  2236.7 18.0 copy-start.1
  (89 other events, 551.2 us)
Sparse Core Ops, SparseCore 0:
  21.6 59.4 all-gather.5
  137.7 56.7 all-gather.11
  196.8 54.2 reduce-scatter.4
  252.5 56.7 all-gather.7
  1674.1 54.3 reduce-scatter.6
  1730.5 56.7 all-gather.9
  1813.7 54.4 reduce-scatter.8
  1935.6 195.4 all-reduce.9
  2134.0 54.1 reduce-scatter.10
where the time goes:
time: 2270 us; the launch traced here: 2260 us
  matrix products  1190 us (52%)
  other arithmetic  460 us (20%)
  waiting for transfers between devices  367 us (16%)
  local copies, waits for them, and re-layouts  189 us (8%)
  blocking collectives  34.2 us (2%)
    dot_general x16, matrix products, masked_scores(): jnp.einsum('gdi,gdj->gij', q_block, key_rows, preferred_element_type=jnp....  378 us
    convert_element_type x8, other arithmetic, one_block(): grad_scores = (prob_f32 * (grad_probs - delta_row)).astype(jnp.bfloat16)  238 us
    dot_general x8, matrix products, one_block(): jnp.einsum('gdi,gdj->gij', g_block, value_rows, preferred_element_type=jn...  147 us
    dot_general x8, matrix products, one_block(): jnp.einsum('gdi,gij->gdj', g_block, probs_low, preferred_element_type=jnp...  134 us
    dot_general x18, matrix products, conv_input_grad(): jnp.einsum('oc,oip->cip', cols_part, moved_grads[kernel_tap], preferred_e...  131 us
    reduce_sum x8, other arithmetic, one_block(): row_total = jnp.sum(raised, axis=-1, keepdims=True)  130 us
    dot_general x8, matrix products, one_block(): jnp.einsum('gdj,gij->gdi', value_rows, probs_low, preferred_element_type=...  128 us
    psum x1, waiting for transfers between devices, local(): lax.psum(conv1_weight_grad.astype(jnp.bfloat16), 'dp').astype(jnp.float32)  119 us
  transfers between devices with their start and end apart: 9, of which 7 were waited for; matrix products, arithmetic and copies ran while one was open for 13% of the time, Pallas kernels for 0%

commit v1 on v0

--- a/solution.py
+++ b/solution.py
@@ -315,7 +315,9 @@
     residual_grads = (
         lax.psum(norm1_gain_grad.astype(jnp.bfloat16), "dp").astype(jnp.float32),
         lax.psum(norm1_bias_grad.astype(jnp.bfloat16), "dp").astype(jnp.float32),
-        lax.psum(conv1_weight_grad.astype(jnp.bfloat16), "dp").astype(jnp.float32),
+        jnp.sum(lax.all_gather(conv1_weight_grad.astype(jnp.bfloat16), "dp"), axis=0).astype(
+            jnp.float32
+        ),
         lax.psum(conv1_bias_grad.astype(jnp.bfloat16), "dp").astype(jnp.float32),
         lax.psum(emb_weight_grad.astype(jnp.bfloat16), "dp").astype(jnp.float32),
         lax.psum(emb_bias_grad.astype(jnp.bfloat16), "dp").astype(jnp.float32),

time: 2270 us -> 2380 us (1.048)
  waiting for transfers between devices: 367 us -> 441 us
  other arithmetic: 460 us -> 487 us
    all_gather x0 -> x1, waiting for transfers between devices: none -> 123 us  [local(): lax.all_gather(conv1_weight_grad.astype(jnp.bfloat16), 'dp')]
    psum x1, waiting for transfers between devices: 119 us -> 66 us  [local(): lax.psum(conv2_weight_grad.astype(jnp.bfloat16), 'dp').astype(jnp.float32)]
    unnamed x235 -> x230, local copies, waits for them, and re-layouts: 68.7 us -> 71.1 us
  transfers between devices with their start and end apart: 9 -> 10, of which waited for: 7 -> 8; matrix products, arithmetic and copies ran while one was open for 13% -> 14% of each run, Pallas kernels for 0% -> 0%
where the time goes in v1:
time: 2380 us; the launch traced here: 2370 us
  matrix products  1190 us (50%)
  other arithmetic  487 us (20%)
  waiting for transfers between devices  441 us (19%)
  local copies, waits for them, and re-layouts  196 us (8%)
  blocking collectives  36.1 us (2%)
    dot_general x16, matrix products, masked_scores(): jnp.einsum('gdi,gdj->gij', q_block, key_rows, preferred_element_type=jnp....  378 us
    convert_element_type x8, other arithmetic, one_block(): grad_scores = (prob_f32 * (grad_probs - delta_row)).astype(jnp.bfloat16)  238 us
    dot_general x8, matrix products, one_block(): jnp.einsum('gdi,gdj->gij', g_block, value_rows, preferred_element_type=jn...  147 us
    dot_general x8, matrix products, one_block(): jnp.einsum('gdi,gij->gdj', g_block, probs_low, preferred_element_type=jnp...  134 us
    reduce_sum x8, other arithmetic, one_block(): row_total = jnp.sum(raised, axis=-1, keepdims=True)  130 us
    dot_general x8, matrix products, one_block(): jnp.einsum('gdj,gij->gdi', value_rows, probs_low, preferred_element_type=...  128 us
    dot_general x18, matrix products, conv_input_grad(): jnp.einsum('oc,oip->cip', cols_part, moved_grads[kernel_tap], preferred_e...  126 us
    all_gather x1, waiting for transfers between devices, local(): lax.all_gather(conv1_weight_grad.astype(jnp.bfloat16), 'dp')  123 us
  transfers between devices with their start and end apart: 10, of which 8 were waited for; matrix products, arithmetic and copies ran while one was open for 14% of the time, Pallas kernels for 0%

profile of v1, /device:TPU:0, one launch (start us, length us, event | category | flops | bytes accessed | tf_op | source)
XLA Modules:
  0.0 2369.9 jit_solution(2276478470253049825)
XLA Ops:
  27.9 53.2 %all-gather.7.cloned.1.call-done = bf16[512,1,4096]{0,2,1:T(8,128)(2,1)} async-done(((bf16[256,1,4096]{0,2,1:T(8,128)(2,1)}), bf16[512,1,4096]{0,2,1:T(8,128)(2,1)}) %all-gather.7.cloned.1.call-update) | async-done | bytes 4194320 | tf_op jit(solution)/shard_map/all_gather | solution.py:203
  81.1 22.0 pad_slice_fusion.8
  132.3 17.8 multiply_convert_fusion.2
  159.5 47.5 %all-gather.15.cloned.1.call-done = bf16[512,4096]{0,1:T(8,128)(2,1)} async-done(((bf16[256,4096]{0,1:T(8,128)(2,1)}), bf16[512,4096]{0,1:T(8,128)(2,1)}) %all-gather.15.cloned.1.call-update) | async-done | bytes 4194320 | tf_op jit(solution)/shard_map/all_gather | solution.py:211
  207.0 21.5 pad_slice_fusion
  269.9 51.9 %all-gather.9.cloned.1.call-done = bf16[512,1,4096]{0,2,1:T(8,128)(2,1)} async-done(((bf16[256,1,4096]{0,2,1:T(8,128)(2,1)}), bf16[512,1,4096]{0,2,1:T(8,128)(2,1)}) %all-gather.9.cloned.1.call-update) | async-done | bytes 4194320 | tf_op jit(solution)/shard_map/all_gather | solution.py:214
  335.3 394.0 %while.30 = (s32[]{:T(128)}, bf16[8,4,64,512]{3,2,1,0:T(8,128)(2,1)}, f32[8,4,512,1]{2,1,3,0:T(4,128)S(1)}, f32[8,4,512,1]{2,1,3,0:T(4,128)S(1)}, bf16[8,4,64,51...) while((s32[]{:T(128)}, ...), condition=%wide.region_15.16_spmd.clone, body=%wide.region_12.15_spmd.clone.sunk | while | flops 2390978560 | bytes 121079936 | solution.py:120
  532.3 17.0 fusion.444
  581.5 17.0 fusion.444
  729.3 921.8 %while.31 = (s32[]{:T(128)}, f32[4,64,4356]{2,1,0:T(8,128)}, f32[4,64,4356]{2,1,0:T(8,128)}, bf16[8,4,64,512]{3,2,1,0:T(8,128)(2,1)}, bf16[8,4,64,512]{3,2,1,0:T...) while((s32[]{:T(128)}, f32[4,64,4356]{2,1,0:T(8,128)}, ...), condition=%wide.region_19.20_spmd.clone, body=%wide.region_17.19_spmd.clone.sunk | while | flops 5804411904 | bytes 302971552 | solution.py:159
  729.5 18.3 fusion.456
  747.8 30.3 %multiply_reduce_fusion.7 = (f32[4,512]{1,0:T(4,128)S(1)}, f32[4,512,4356]{1,2,0:T(8,128)}) fusion(f32[4,512,4356]{1,2,0:T(8,128)} %fusion.456, f32[4,512]{1,0:T(4,128)S(1)} %get-tuple-element.527, f32[4,512]{1,0:T(4,128)S(1)} %get-tuple-element.528, bf16[4,64,4356]{2,1,0:T(8,128)(2,1)} %get-tuple-element.589, ...), kind=kOutput, calls=%fused_computation.20.clone.1 | convolution fusion | flops 1195423744 | bytes 73890816 | tf_op jit(solution)/shard_map/while/body/eval_jaxpr/gdi,gdj->gij/dot_general | solution.py:98
  778.1 29.7 %multiply_convert_fusion.4 = bf16[4,512,4356]{1,2,0:T(8,128)(2,1)} fusion(f32[4,512,4356]{1,2,0:T(8,128)} %get-tuple-element.529, f32[4,512,4356]{1,2,0:T(8,128)} %fusion.456, f32[4,512]{1,0:T(4,128)S(1)} %get-tuple-element.530), kind=kLoop, calls=%fused_computation.19.clone.1 | loop fusion | flops 26763264 | bytes 89219072 | tf_op jit(solution)/shard_map/while/body/eval_jaxpr/convert_element_type | solution.py:146
  842.1 18.3 fusion.456
  860.4 30.3 %multiply_reduce_fusion.7 = (f32[4,512]{1,0:T(4,128)S(1)}, f32[4,512,4356]{1,2,0:T(8,128)}) fusion(f32[4,512,4356]{1,2,0:T(8,128)} %fusion.456, f32[4,512]{1,0:T(4,128)S(1)} %get-tuple-element.527, f32[4,512]{1,0:T(4,128)S(1)} %get-tuple-element.528, bf16[4,64,4356]{2,1,0:T(8,128)(2,1)} %get-tuple-element.589, ...), kind=kOutput, calls=%fused_computation.20.clone.1 | convolution fusion | flops 1195423744 | bytes 73890816 | tf_op jit(solution)/shard_map/while/body/eval_jaxpr/gdi,gdj->gij/dot_general | solution.py:98
  890.7 29.7 %multiply_convert_fusion.4 = bf16[4,512,4356]{1,2,0:T(8,128)(2,1)} fusion(f32[4,512,4356]{1,2,0:T(8,128)} %get-tuple-element.529, f32[4,512,4356]{1,2,0:T(8,128)} %fusion.456, f32[4,512]{1,0:T(4,128)S(1)} %get-tuple-element.530), kind=kLoop, calls=%fused_computation.19.clone.1 | loop fusion | flops 26763264 | bytes 89219072 | tf_op jit(solution)/shard_map/while/body/eval_jaxpr/convert_element_type | solution.py:146
  940.6 17.0 fusion.458
  957.6 18.3 fusion.456
  976.0 30.3 %multiply_reduce_fusion.7 = (f32[4,512]{1,0:T(4,128)S(1)}, f32[4,512,4356]{1,2,0:T(8,128)}) fusion(f32[4,512,4356]{1,2,0:T(8,128)} %fusion.456, f32[4,512]{1,0:T(4,128)S(1)} %get-tuple-element.527, f32[4,512]{1,0:T(4,128)S(1)} %get-tuple-element.528, bf16[4,64,4356]{2,1,0:T(8,128)(2,1)} %get-tuple-element.589, ...), kind=kOutput, calls=%fused_computation.20.clone.1 | convolution fusion | flops 1195423744 | bytes 73890816 | tf_op jit(solution)/shard_map/while/body/eval_jaxpr/gdi,gdj->gij/dot_general | solution.py:98
  1006.2 29.7 %multiply_convert_fusion.4 = bf16[4,512,4356]{1,2,0:T(8,128)(2,1)} fusion(f32[4,512,4356]{1,2,0:T(8,128)} %get-tuple-element.529, f32[4,512,4356]{1,2,0:T(8,128)} %fusion.456, f32[4,512]{1,0:T(4,128)S(1)} %get-tuple-element.530), kind=kLoop, calls=%fused_computation.19.clone.1 | loop fusion | flops 26763264 | bytes 89219072 | tf_op jit(solution)/shard_map/while/body/eval_jaxpr/convert_element_type | solution.py:146
  1056.1 17.0 fusion.458
  1073.1 18.3 fusion.456
  1091.5 30.3 %multiply_reduce_fusion.7 = (f32[4,512]{1,0:T(4,128)S(1)}, f32[4,512,4356]{1,2,0:T(8,128)}) fusion(f32[4,512,4356]{1,2,0:T(8,128)} %fusion.456, f32[4,512]{1,0:T(4,128)S(1)} %get-tuple-element.527, f32[4,512]{1,0:T(4,128)S(1)} %get-tuple-element.528, bf16[4,64,4356]{2,1,0:T(8,128)(2,1)} %get-tuple-element.589, ...), kind=kOutput, calls=%fused_computation.20.clone.1 | convolution fusion | flops 1195423744 | bytes 73890816 | tf_op jit(solution)/shard_map/while/body/eval_jaxpr/gdi,gdj->gij/dot_general | solution.py:98
  1121.8 29.7 %multiply_convert_fusion.4 = bf16[4,512,4356]{1,2,0:T(8,128)(2,1)} fusion(f32[4,512,4356]{1,2,0:T(8,128)} %get-tuple-element.529, f32[4,512,4356]{1,2,0:T(8,128)} %fusion.456, f32[4,512]{1,0:T(4,128)S(1)} %get-tuple-element.530), kind=kLoop, calls=%fused_computation.19.clone.1 | loop fusion | flops 26763264 | bytes 89219072 | tf_op jit(solution)/shard_map/while/body/eval_jaxpr/convert_element_type | solution.py:146
  1171.7 17.0 fusion.458
  1188.7 18.3 fusion.456
  1207.0 30.3 %multiply_reduce_fusion.7 = (f32[4,512]{1,0:T(4,128)S(1)}, f32[4,512,4356]{1,2,0:T(8,128)}) fusion(f32[4,512,4356]{1,2,0:T(8,128)} %fusion.456, f32[4,512]{1,0:T(4,128)S(1)} %get-tuple-element.527, f32[4,512]{1,0:T(4,128)S(1)} %get-tuple-element.528, bf16[4,64,4356]{2,1,0:T(8,128)(2,1)} %get-tuple-element.589, ...), kind=kOutput, calls=%fused_computation.20.clone.1 | convolution fusion | flops 1195423744 | bytes 73890816 | tf_op jit(solution)/shard_map/while/body/eval_jaxpr/gdi,gdj->gij/dot_general | solution.py:98
  1237.3 29.7 %multiply_convert_fusion.4 = bf16[4,512,4356]{1,2,0:T(8,128)(2,1)} fusion(f32[4,512,4356]{1,2,0:T(8,128)} %get-tuple-element.529, f32[4,512,4356]{1,2,0:T(8,128)} %fusion.456, f32[4,512]{1,0:T(4,128)S(1)} %get-tuple-element.530), kind=kLoop, calls=%fused_computation.19.clone.1 | loop fusion | flops 26763264 | bytes 89219072 | tf_op jit(solution)/shard_map/while/body/eval_jaxpr/convert_element_type | solution.py:146
  1287.2 17.0 fusion.458
  1304.2 18.3 fusion.456
  1322.5 30.3 %multiply_reduce_fusion.7 = (f32[4,512]{1,0:T(4,128)S(1)}, f32[4,512,4356]{1,2,0:T(8,128)}) fusion(f32[4,512,4356]{1,2,0:T(8,128)} %fusion.456, f32[4,512]{1,0:T(4,128)S(1)} %get-tuple-element.527, f32[4,512]{1,0:T(4,128)S(1)} %get-tuple-element.528, bf16[4,64,4356]{2,1,0:T(8,128)(2,1)} %get-tuple-element.589, ...), kind=kOutput, calls=%fused_computation.20.clone.1 | convolution fusion | flops 1195423744 | bytes 73890816 | tf_op jit(solution)/shard_map/while/body/eval_jaxpr/gdi,gdj->gij/dot_general | solution.py:98
  1352.8 29.7 %multiply_convert_fusion.4 = bf16[4,512,4356]{1,2,0:T(8,128)(2,1)} fusion(f32[4,512,4356]{1,2,0:T(8,128)} %get-tuple-element.529, f32[4,512,4356]{1,2,0:T(8,128)} %fusion.456, f32[4,512]{1,0:T(4,128)S(1)} %get-tuple-element.530), kind=kLoop, calls=%fused_computation.19.clone.1 | loop fusion | flops 26763264 | bytes 89219072 | tf_op jit(solution)/shard_map/while/body/eval_jaxpr/convert_element_type | solution.py:146
  1402.7 17.0 fusion.458
  1419.7 18.3 fusion.456
  1438.1 30.3 %multiply_reduce_fusion.7 = (f32[4,512]{1,0:T(4,128)S(1)}, f32[4,512,4356]{1,2,0:T(8,128)}) fusion(f32[4,512,4356]{1,2,0:T(8,128)} %fusion.456, f32[4,512]{1,0:T(4,128)S(1)} %get-tuple-element.527, f32[4,512]{1,0:T(4,128)S(1)} %get-tuple-element.528, bf16[4,64,4356]{2,1,0:T(8,128)(2,1)} %get-tuple-element.589, ...), kind=kOutput, calls=%fused_computation.20.clone.1 | convolution fusion | flops 1195423744 | bytes 73890816 | tf_op jit(solution)/shard_map/while/body/eval_jaxpr/gdi,gdj->gij/dot_general | solution.py:98
  1468.4 29.7 %multiply_convert_fusion.4 = bf16[4,512,4356]{1,2,0:T(8,128)(2,1)} fusion(f32[4,512,4356]{1,2,0:T(8,128)} %get-tuple-element.529, f32[4,512,4356]{1,2,0:T(8,128)} %fusion.456, f32[4,512]{1,0:T(4,128)S(1)} %get-tuple-element.530), kind=kLoop, calls=%fused_computation.19.clone.1 | loop fusion | flops 26763264 | bytes 89219072 | tf_op jit(solution)/shard_map/while/body/eval_jaxpr/convert_element_type | solution.py:146
  1518.2 17.0 fusion.458
  1535.2 18.3 fusion.456
  1553.6 30.3 %multiply_reduce_fusion.7 = (f32[4,512]{1,0:T(4,128)S(1)}, f32[4,512,4356]{1,2,0:T(8,128)}) fusion(f32[4,512,4356]{1,2,0:T(8,128)} %fusion.456, f32[4,512]{1,0:T(4,128)S(1)} %get-tuple-element.527, f32[4,512]{1,0:T(4,128)S(1)} %get-tuple-element.528, bf16[4,64,4356]{2,1,0:T(8,128)(2,1)} %get-tuple-element.589, ...), kind=kOutput, calls=%fused_computation.20.clone.1 | convolution fusion | flops 1195423744 | bytes 73890816 | tf_op jit(solution)/shard_map/while/body/eval_jaxpr/gdi,gdj->gij/dot_general | solution.py:98
  1583.9 29.7 %multiply_convert_fusion.4 = bf16[4,512,4356]{1,2,0:T(8,128)(2,1)} fusion(f32[4,512,4356]{1,2,0:T(8,128)} %get-tuple-element.529, f32[4,512,4356]{1,2,0:T(8,128)} %fusion.456, f32[4,512]{1,0:T(4,128)S(1)} %get-tuple-element.530), kind=kLoop, calls=%fused_computation.19.clone.1 | loop fusion | flops 26763264 | bytes 89219072 | tf_op jit(solution)/shard_map/while/body/eval_jaxpr/convert_element_type | solution.py:146
  1633.7 17.0 fusion.458
  1695.5 45.2 %reduce-scatter.7.cloned.1.call-done = bf16[256,1,4096]{0,2,1:T(8,128)(2,1)} async-done(((bf16[512,1,4096]{0,2,1:T(8,128)(2,1)}), bf16[256,1,4096]{0,2,1:T(8,128)(2,1)}) %reduce-scatter.7.cloned.1.call-update) | async-done | bytes 2097168 | tf_op jit(solution)/shard_map/reduce_scatter | solution.py:276
  1801.4 24.3 %fusion.43 = bf16[512,1,4096]{0,2,1:T(8,128)(2,1)} fusion(bf16[256,4096]{0,1:T(8,128)(2,1)} %bitcast.785, f32[4096,512]{1,0:T(8,128)} %fusion.338, f32[4096,512]{1,0:T(8,128)} %fusion.337, f32[4096,512]{1,0:T(8,128)} %fusion.336, f32[4096,512]{1,0:T(8,128)} %fusion.133, f32[4096,512]{1,0:T(8,128)} %fusion.335, f32[4096,512]{1,0:T(8,128)} %fusion.334, ...), kind=kOutput, calls=%fused_computation.63 | convolution fusion | flops 1092616192 | bytes 73662464 | tf_op jit(solution)/shard_map/oc,oip->cip/dot_general | solution.py:70
  1948.4 25.2 %fusion.44 = bf16[512,1,4096]{0,2,1:T(8,128)(2,1)} fusion(bf16[256,4096]{0,1:T(8,128)(2,1)} %bitcast.784, f32[4096,512]{1,0:T(8,128)} %fusion.331, f32[4096,512]{1,0:T(8,128)} %fusion.330, f32[4096,512]{1,0:T(8,128)} %fusion.329, f32[4096,512]{1,0:T(8,128)} %fusion.113, f32[4096,512]{1,0:T(8,128)} %fusion.328, f32[4096,512]{1,0:T(8,128)} %fusion.327, ...), kind=kOutput, calls=%fused_computation.64 | convolution fusion | flops 1092616192 | bytes 73662464 | tf_op jit(solution)/shard_map/oc,oip->cip/dot_general | solution.py:70
  2025.1 66.0 %all-reduce.10.cloned.1.call-done = (bf16[256,4608]{0,1:T(8,128)(2,1)}, bf16[256,512]{0,1:T(8,128)(2,1)}, bf16[2,2048,256]{2,1,0:T(8,128)(2,1)}, bf16[3,256,512]{2,1,0:T(8,128)(2,1)}, bf16[2,256,2048]{2,1,0:T(8,128)(2,1)}) async-done(((bf16[256,4608]{0,1:T(8,128)(2,1)}, bf16[256,512]{0,1:T(8,128)(2,1)}, bf16[2,2048,256]{2,1,0:T(8,128)(2,1)}, bf16[3,256,512]{2,1,0:T(8,128)(2,1)}, ...) | async-done | bytes 7602192 | tf_op jit(solution)/shard_map/psum | solution.py:326
  2103.0 45.0 %reduce-scatter.11.cloned.1.call-done = bf16[256,1,4096]{0,2,1:T(8,128)(2,1)} async-done(((bf16[512,1,4096]{0,2,1:T(8,128)(2,1)}), bf16[256,1,4096]{0,2,1:T(8,128)(2,1)}) %reduce-scatter.11.cloned.1.call-update) | async-done | bytes 2097168 | tf_op jit(solution)/shard_map/reduce_scatter | solution.py:73
  2154.0 36.1 %all-reduce.6 = (bf16[256]{0:T(256)(128)(2,1)S(1)}, bf16[256]{0:T(256)(128)(2,1)S(1)}, bf16[256]{0:T(256)(128)(2,1)S(1)}, bf16[2,256]{1,0:T(2,128)(2,1)S(1)}, bf...) all-reduce(bf16[256]{0:T(256)(128)(2,1)S(1)} %get-tuple-element.272, ...), channel_id=1, replica_groups=mesh['dp'=16,'tensor'=2] {'dp'}, use_global_device_ids=true, to_apply=%region_42.43 | all-reduce | flops 4096 | bytes 16384 | tf_op jit(solution)/shard_map/psum | solution.py:316
  2216.0 123.0 %all-gather.13.cloned.1.call-done = bf16[16,256,4608]{2,1,0:T(8,128)(2,1)} async-done(((bf16[1,256,4608]{2,1,0:T(8,128)(2,1)}), bf16[16,256,4608]{2,1,0:T(8,128)(2,1)}) %all-gather.13.cloned.1.call-update) | async-done | bytes 37748752 | tf_op jit(solution)/shard_map/all_gather | solution.py:318
  (539 shorter events, 994.3 us)
Async XLA Ops:
  7.2 255.8 %copy-start = (bf16[2,256,2048]{2,1,0:T(8,128)(2,1)S(1)}, bf16[2,256,2048]{2,1,0:T(8,128)(2,1)}, u32[]{:S(2)}) copy-start(bf16[2,256,2048]{2,1,0:T(8,128)(2,1)} %param.46) | copy-start | bytes 6291460
  7.2 73.9 %all-gather.7.cloned.1.call-start = ((), (), s32[]{:S(2)}) async-start(), calls=%async_computation.4 | async-start | bytes 6291456 | tf_op jit(solution)/shard_map/all_gather | solution.py:203
  21.6 185.4 %all-gather.15.cloned.1.call-start = ((), (), s32[]{:S(2)}) async-start(), calls=%async_computation.12 | async-start | bytes 6291456 | tf_op jit(solution)/shard_map/all_gather | solution.py:211
  27.9 104.3 %copy-start.69 = (f32[1,256]{1,0:T(1,128)}, f32[1,256]{1,0:T(1,128)S(1)}, u32[]{:S(2)}) copy-start(f32[1,256]{1,0:T(1,128)S(1)} %get-tuple-element.389) | copy-start | bytes 3076
  27.9 104.3 %copy-start.85 = (f32[1,256]{1,0:T(1,128)}, f32[1,256]{1,0:T(1,128)S(1)}, u32[]{:S(2)}) copy-start(f32[1,256]{1,0:T(1,128)S(1)} %get-tuple-element.390) | copy-start | bytes 3076
  81.1 22.0 copy-start.94
  103.1 17.8 copy-start.17
  103.1 19.1 copy-start.15
  103.1 20.5 copy-start.13
  103.2 21.8 copy-start.11
  128.6 21.5 copy-start.63
  132.2 17.9 copy-start.67
  132.3 17.9 copy-start.54
  150.1 116.1 %reduce-scatter.5.cloned.1.call-start = ((), (), s32[]{:S(2)}) async-start(), calls=%async_computation.7 | async-start | bytes 6291456 | tf_op jit(solution)/shard_map/reduce_scatter | solution.py:246
  155.0 166.8 %all-gather.9.cloned.1.call-start = ((), (), s32[]{:S(2)}) async-start(), calls=%async_computation.5 | async-start | bytes 6291456 | tf_op jit(solution)/shard_map/all_gather | solution.py:214
  207.0 21.5 copy-start.95
  228.5 18.1 copy-start.31
  228.5 19.5 copy-start.29
  228.5 20.8 copy-start.27
  228.5 22.1 copy-start.7
  262.8 1477.9 %reduce-scatter.7.cloned.1.call-start = ((), (), s32[]{:S(2)}) async-start(), calls=%async_computation.8 | async-start | bytes 6291456 | tf_op jit(solution)/shard_map/reduce_scatter | solution.py:276
  263.0 58.8 %copy-start.107 = (bf16[3,256,512]{2,1,0:T(8,128)(2,1)S(1)}, bf16[3,256,512]{2,1,0:T(8,128)(2,1)}, u32[]{:S(2)}) copy-start(bf16[3,256,512]{2,1,0:T(8,128)(2,1)} %param.44) | copy-start | bytes 2359300
  263.0 58.8 %copy-start.109 = (f32[3,256]{1,0:T(4,128)S(1)}, f32[3,256]{1,0:T(4,128)}, u32[]{:S(2)}) copy-start(f32[3,256]{1,0:T(4,128)} %param.45) | copy-start | bytes 9220
  352.2 16.3 copy-start.6
  1686.3 154.7 %all-gather.11.cloned.1.call-start = ((), (), s32[]{:S(2)}) async-start(), calls=%async_computation.6 | async-start | bytes 6291456 | tf_op jit(solution)/shard_map/all_gather | solution.py:234
  1693.1 47.7 %copy-start.59 = (f32[256]{0:T(256)S(1)}, f32[256]{0:T(256)}, u32[]{:S(2)}) copy-start(f32[256]{0:T(256)} %copy-done.58) | copy-start | bytes 3076
  1693.1 47.7 %copy-start.72 = (f32[256]{0:T(256)S(1)}, f32[256]{0:T(256)}, u32[]{:S(2)}) copy-start(f32[256]{0:T(256)} %copy-done.71) | copy-start | bytes 3076
  1693.1 47.7 %copy-start.81 = (f32[256]{0:T(256)S(1)}, f32[256]{0:T(256)}, u32[]{:S(2)}) copy-start(f32[256]{0:T(256)} %param.42) | copy-start | bytes 3076
  1695.5 50.2 %copy-start.106 = (f32[16]{0:T(128)S(1)}, f32[16]{0:T(128)}, u32[]{:S(2)}) copy-start(f32[16]{0:T(128)} %copy-done.105) | copy-start | bytes 196
  1695.5 184.9 %reduce-scatter.9.cloned.1.call-start = ((), (), s32[]{:S(2)}) async-start(), calls=%async_computation.9 | async-start | bytes 6291456 | tf_op jit(solution)/shard_map/reduce_scatter | solution.py:73
  1825.8 265.2 %all-reduce.10.cloned.1.call-start = ((), (), s32[]{:S(2)}) async-start(), calls=%async_computation.13 | async-start | bytes 15204352 | tf_op jit(solution)/shard_map/psum | solution.py:326
  1871.4 16.5 copy-start.104
  1930.6 217.5 %reduce-scatter.11.cloned.1.call-start = ((), (), s32[]{:S(2)}) async-start(), calls=%async_computation.10 | async-start | bytes 6291456 | tf_op jit(solution)/shard_map/reduce_scatter | solution.py:73
  1973.7 365.4 %all-gather.13.cloned.1.call-start = ((), (), s32[]{:S(2)}) async-start(), calls=%async_computation.11 | async-start | bytes 40108032 | tf_op jit(solution)/shard_map/all_gather | solution.py:318
  2098.0 50.0 %copy-start.5 = (bf16[256,1,4096]{0,2,1:T(8,128)(2,1)S(1)}, bf16[256,1,4096]{0,2,1:T(8,128)(2,1)}, u32[]{:S(2)}) copy-start(bf16[256,1,4096]{0,2,1:T(8,128)(2,1)} %copy.149) | copy-start | bytes 6291460
  2098.1 50.0 %copy-start.62 = (f32[256]{0:T(256)S(1)}, f32[256]{0:T(256)}, u32[]{:S(2)}) copy-start(f32[256]{0:T(256)} %copy-done.61) | copy-start | bytes 3076
  2098.1 50.0 %copy-start.75 = (f32[256]{0:T(256)S(1)}, f32[256]{0:T(256)}, u32[]{:S(2)}) copy-start(f32[256]{0:T(256)} %copy-done.74) | copy-start | bytes 3076
  2098.1 50.0 %copy-start.84 = (f32[256]{0:T(256)S(1)}, f32[256]{0:T(256)}, u32[]{:S(2)}) copy-start(f32[256]{0:T(256)} %param.32) | copy-start | bytes 3076
  2098.1 50.0 %copy-start.93 = (f32[256]{0:T(256)S(1)}, f32[256]{0:T(256)}, u32[]{:S(2)}) copy-start(f32[256]{0:T(256)} %param.33) | copy-start | bytes 3076
  2103.0 51.0 %copy-start.96 = (bf16[256]{0:T(256)(128)(2,1)S(1)}, bf16[256]{0:T(256)(128)(2,1)}, u32[]{:S(2)}) copy-start(bf16[256]{0:T(256)(128)(2,1)} %get-tuple-element.270) | copy-start | bytes 1540
  2103.0 51.0 %copy-start.98 = (bf16[256]{0:T(256)(128)(2,1)S(1)}, bf16[256]{0:T(256)(128)(2,1)}, u32[]{:S(2)}) copy-start(bf16[256]{0:T(256)(128)(2,1)} %get-tuple-element.337) | copy-start | bytes 1540
  2103.0 51.0 %copy-start.99 = (bf16[256]{0:T(256)(128)(2,1)S(1)}, bf16[256]{0:T(256)(128)(2,1)}, u32[]{:S(2)}) copy-start(bf16[256]{0:T(256)(128)(2,1)} %get-tuple-element.370) | copy-start | bytes 1540
  2103.0 94.1 %copy-start.102 = (f32[16]{0:T(128)S(1)}, f32[16]{0:T(128)}, u32[]{:S(2)}) copy-start(f32[16]{0:T(128)} %copy-done.101) | copy-start | bytes 196
  2103.0 95.4 %copy-start.60 = (f32[256]{0:T(256)S(1)}, f32[256]{0:T(256)}, u32[]{:S(2)}) copy-start(f32[256]{0:T(256)} %copy-done.58) | copy-start | bytes 3076
  2103.0 95.4 %copy-start.73 = (f32[256]{0:T(256)S(1)}, f32[256]{0:T(256)}, u32[]{:S(2)}) copy-start(f32[256]{0:T(256)} %copy-done.71) | copy-start | bytes 3076
  2103.0 95.4 %copy-start.79 = (f32[256]{0:T(256)S(1)}, f32[256]{0:T(256)}, u32[]{:S(2)}) copy-start(f32[256]{0:T(256)} %copy-done.78) | copy-start | bytes 3076
  2103.0 95.4 %copy-start.82 = (f32[256]{0:T(256)S(1)}, f32[256]{0:T(256)}, u32[]{:S(2)}) copy-start(f32[256]{0:T(256)} %param.42) | copy-start | bytes 3076
  2103.0 95.4 %copy-start.88 = (f32[256]{0:T(256)S(1)}, f32[256]{0:T(256)}, u32[]{:S(2)}) copy-start(f32[256]{0:T(256)} %copy-done.87) | copy-start | bytes 3076
  (87 other events, 579.0 us)
Sparse Core Ops, SparseCore 0:
  21.7 59.4 all-gather.6
  150.2 56.7 all-gather.14
  209.3 54.2 reduce-scatter.4
  265.0 56.7 all-gather.8
  1686.5 54.2 reduce-scatter.6
  1742.7 56.7 all-gather.10
  1825.9 54.4 reduce-scatter.8
  1930.7 160.2 all-reduce.9
  2093.9 54.1 reduce-scatter.10
  2149.6 189.4 all-gather.12
